TPU v7x, 512 devices: a whole 4x4x16 slice. The times are simulated.
512 devices in a mesh: prow: 16 (over x, y), pcol: 32 (over z, core).
Axes of the slice: x: 4, y: 4, z: 16, core: 2. Of those that a mesh axis runs over, the one named last changes fastest.
Arguments:
- adjoint_trail: float32 [2, 16, 256, 1, 32, 256], P(None, 'prow', None, None, 'pcol'), as said below
- factor_low: float32 [2, 16, 32, 8, 4, 256], P(None, 'prow', 'pcol'), may hold values from -0.0625 to 0.0625
- adjoint_low: float32 [2, 16, 32, 8, 4, 256], P(None, 'prow', 'pcol'), may hold values from -6 to 6
- factor_top: float32 [10, 256, 256], P(None, 'pcol'), as said below
- adjoint_top: float32 [10, 256, 256], P(None, 'pcol'), may hold values from -6 to 6
- diag_inverse: float32 [4, 256, 256], P(None, 'pcol'), as said below
Outputs:
- grad_low: float32 [2, 16, 32, 8, 4, 256], P(None, 'prow', 'pcol')
- grad_top: float32 [10, 256, 256], P(None, 'pcol')
Inputs may be any that keep to these rules, and one draw needn't show every extreme that they name: adjoint_trail reshaped row-major to 8192 x 8192 is symmetric. The diagonal blocks factor_top[j (j + 1) / 2 + j] are lower triangular with a positive diagonal. diag_inverse[j] is the inverse of factor_top[j (j + 1) / 2 + j].
All inputs are finite; a program needn't handle non-finite values.
Results may differ from a plain program's by a relative error of at most 0.00024.
Values sent between devices are 32-bit elements; how exact they have to be, the bound alone decides.
A program may use at most 64 MiB of HBM per device.

v0:
```python
import jax
import jax.numpy as jnp
from jax import lax
from jax.sharding import PartitionSpec as P

NB = 256
K = 4
HIGHEST = lax.Precision.HIGHEST


def from_root(array, axis, root):
    mine = lax.axis_index(axis) == root
    return lax.psum(jnp.where(mine, array, jnp.zeros_like(array)), axis)


def matmul(left, right):
    return jnp.dot(left, right, precision=HIGHEST, preferred_element_type=jnp.float32)


def inner_product(left, right):
    return lax.dot_general(
        left, right, (((0,), (0,)), ((), ())), precision=HIGHEST, preferred_element_type=jnp.float32
    )


def block_slot(row_block, col_block):
    return row_block * (row_block + 1) // 2 + col_block


def half_lower(square):
    size = square.shape[0]
    row_ids = lax.broadcasted_iota(jnp.int32, (size, size), 0)
    col_ids = lax.broadcasted_iota(jnp.int32, (size, size), 1)
    return jnp.where(row_ids > col_ids, square, jnp.where(row_ids == col_ids, 0.5 * square, 0.0))


def diagonal_adjoint(diagonal, inverse, lower_adj):
    inner = half_lower(inner_product(jnp.tril(diagonal), lower_adj))
    spread = inner_product(inverse, matmul(inner, inverse))
    return 0.5 * (spread + spread.T)


def rows_one(piece):
    return lax.all_gather(piece, "pcol", axis=1, tiled=True)


def owner_one(piece, root):
    return from_root(piece, "prow", root)


def reduce_one(term, count):
    return lax.psum_scatter(
        term(jnp.int32(0), lax.axis_size("pcol") * count), "pcol", scatter_dimension=0, tiled=True
    )


def trailing_product(trail, panels, gather_rows, send_owner, reduce_rows):
    prow_count = lax.axis_size("prow")
    pcol_count = lax.axis_size("pcol")
    cycles, sub_rows, width = panels.shape
    block = sub_rows * pcol_count
    gathered = gather_rows(panels[:, None]).reshape(cycles, block, width)
    column = lax.axis_index("pcol")
    col_cycles = trail.shape[3]
    global_block = 0 + column
    share = lax.dynamic_index_in_dim(gathered, global_block // prow_count, 0, keepdims=False)
    owned = [send_owner(share, global_block % prow_count)]
    stacked = jnp.stack(owned)
    view = trail.reshape(cycles, pcol_count, sub_rows, col_cycles, block)
    unit = cycles * sub_rows

    def term(start, count):
        product = jnp.einsum(
            "iaekb,kbn->aien", view, stacked, precision=HIGHEST, preferred_element_type=jnp.float32
        )
        return product.reshape(count, width)

    return reduce_rows(term, unit).reshape(cycles, sub_rows, width)


def per_device(adjoint_trail, factor_low, adjoint_low, factor_top, adjoint_top, diag_inverse):
    cycles = factor_low.shape[0]
    sub_rows = factor_low.shape[3]
    local_rows = cycles * sub_rows
    low_factor = factor_low.reshape(cycles, sub_rows, K * NB)
    low_adjoint = adjoint_low.reshape(local_rows, K, NB)
    columns = low_factor.reshape(local_rows, K, NB)
    top_factor, top_adjoint, inverses = (
        lax.all_gather(factor_top, "pcol", axis=1, tiled=True),
        lax.all_gather(adjoint_top, "pcol", axis=1, tiled=True),
        lax.all_gather(diag_inverse, "pcol", axis=1, tiled=True),
    )
    lower_grads = [None] * K
    diag_grads = [None] * K
    upper_grads = {}
    grams = {}

    def lower_step(panel):
        single = low_factor[:, :, panel * NB : (panel + 1) * NB]
        image = trailing_product(adjoint_trail, single, rows_one, owner_one, reduce_one).reshape(
            local_rows, NB
        )
        residual = low_adjoint[:, panel] - 2.0 * image
        for later in range(panel + 1, K):
            residual = residual - matmul(lower_grads[later], top_factor[block_slot(later, panel)])
        lower_grads[panel] = matmul(residual, inverses[panel])

    def top_step(panel):
        for row_block in range(panel + 1, K):
            top_residual = top_adjoint[block_slot(row_block, panel)] - grams[row_block, panel]
            top_residual = top_residual - 2.0 * matmul(
                diag_grads[row_block], top_factor[block_slot(row_block, panel)]
            )
            for middle in range(panel + 1, row_block):
                top_residual = top_residual - matmul(
                    upper_grads[middle, row_block], top_factor[block_slot(middle, panel)]
                )
            for beyond in range(row_block + 1, K):
                top_residual = top_residual - inner_product(
                    upper_grads[row_block, beyond], top_factor[block_slot(beyond, panel)]
                )
            upper_grads[panel, row_block] = matmul(top_residual, inverses[panel])
        lower_adj = top_adjoint[block_slot(panel, panel)] - grams[panel, panel]
        for row_block in range(panel + 1, K):
            lower_adj = lower_adj - inner_product(
                upper_grads[panel, row_block], top_factor[block_slot(row_block, panel)]
            )
        diag_grads[panel] = diagonal_adjoint(
            top_factor[block_slot(panel, panel)], inverses[panel], jnp.tril(lower_adj)
        )

    for panel in reversed(range(K)):
        lower_step(panel)
        local_gram = jnp.stack(
            [inner_product(lower_grads[panel], columns[:, earlier]) for earlier in range(panel + 1)]
        )
        summed = lax.psum(local_gram, ("prow", "pcol"))
        for earlier in range(panel + 1):
            grams[panel, earlier] = summed[earlier]
        top_step(panel)
    grad_low = jnp.stack(lower_grads, 1).reshape(factor_low.shape)
    blocks = []
    for row_block in range(K):
        for col_block in range(row_block + 1):
            if row_block == col_block:
                blocks.append(diag_grads[col_block])
            else:
                blocks.append(upper_grads[col_block, row_block])
    full_top = jnp.stack(blocks)
    share_rows = factor_top.shape[1]
    grad_top = lax.dynamic_slice_in_dim(
        full_top, lax.axis_index("pcol") * share_rows, share_rows, 1
    )
    return (grad_low, grad_top)


def solution(mesh):
    in_specs = (
        P(None, "prow", None, None, "pcol", None),
        P(None, "prow", "pcol", None, None, None),
        P(None, "prow", "pcol", None, None, None),
        P(None, "pcol", None),
        P(None, "pcol", None),
        P(None, "pcol", None),
    )
    out_specs = (P(None, "prow", "pcol", None, None, None), P(None, "pcol", None))
    return jax.shard_map(
        per_device, mesh=mesh, in_specs=in_specs, out_specs=out_specs, check_vma=False
    )
```

profile of v0, /device:TPU:8, one launch (start us, length us, event | category | flops | bytes accessed | tf_op | source)
XLA Modules:
  0.0 1294.8 jit_solution(6312719842912323253)
XLA Ops:
  9.0 37.8 %all-gather.3 = f32[2,256,256]{2,1,0:T(8,128)S(1)} all-gather(f32[2,8,256]{2,1,0:T(8,128)S(1)} %get-tuple-element.15), channel_id=5, replica_groups=mesh['prow'=16,'pcol'=32] {'pcol'}, dimensions={1}, use_global_device_ids=true | all-gather | bytes 540672 | tf_op jit(solution)/shard_map/all_gather | solution.py:44
  46.8 28.5 %all-gather.2 = f32[2,256,256]{2,1,0:T(8,128)S(1)} all-gather(f32[2,8,256]{2,1,0:T(8,128)S(1)} %get-tuple-element.16), channel_id=4, replica_groups=mesh['prow'=16,'pcol'=32] {'pcol'}, dimensions={1}, use_global_device_ids=true | all-gather | bytes 540672 | tf_op jit(solution)/shard_map/all_gather | solution.py:44
  76.7 29.8 %all-gather.1 = f32[2,256,256]{2,1,0:T(8,128)S(1)} all-gather(f32[2,8,256]{2,1,0:T(8,128)S(1)} %get-tuple-element.17), channel_id=3, replica_groups=mesh['prow'=16,'pcol'=32] {'pcol'}, dimensions={1}, use_global_device_ids=true | all-gather | bytes 540672 | tf_op jit(solution)/shard_map/all_gather | solution.py:44
  107.3 28.5 %all-gather = f32[2,256,256]{2,1,0:T(8,128)S(1)} all-gather(f32[2,8,256]{2,1,0:T(8,128)S(1)} %get-tuple-element.14), channel_id=2, replica_groups=mesh['prow'=16,'pcol'=32] {'pcol'}, dimensions={1}, use_global_device_ids=true | all-gather | bytes 540672 | tf_op jit(solution)/shard_map/all_gather | solution.py:44
  137.2 113.6 %all-reduce.7.cloned.1.call-done = (f32[256,256]{1,0:T(8,128)}, f32[256,256]{1,0:T(8,128)}, f32[256,256]{1,0:T(8,128)}, f32[256,256]{1,0:T(8,128)}) async-done(((f32[256,256]{1,0:T(8,128)}, f32[256,256]{1,0:T(8,128)}, f32[256,256]{1,0:T(8,128)}, f32[256,256]{1,0:T(8,128)}), (f32[256,256]{1,0:T(8,128)}, f32[256,256]{1,0:T(8,128)}, f32[256,256]{1,0:T(8,128)}, ...) | async-done | bytes 1048592 | tf_op jit(solution)/shard_map/psum | solution.py:13
  250.9 1.7 convolution_bitcast_fusion
  261.1 99.8 %reduce-scatter.11.cloned.1.call-done = f32[16,256]{1,0:T(8,128)} async-done(((f32[512,256]{1,0:T(8,128)}), f32[16,256]{1,0:T(8,128)}) %reduce-scatter.11.cloned.1.call-update) | async-done | bytes 16400 | tf_op jit(solution)/shard_map/reduce_scatter | solution.py:52
  364.8 104.2 %reduce-scatter.9.cloned.1.call-done = f32[16,256]{1,0:T(8,128)} async-done(((f32[512,256]{1,0:T(8,128)}), f32[16,256]{1,0:T(8,128)}) %reduce-scatter.9.cloned.1.call-update) | async-done | bytes 16400 | tf_op jit(solution)/shard_map/reduce_scatter | solution.py:52
  469.0 72.4 %all-gather.10.cloned.1.call-done = f32[10,256,256]{2,1,0:T(8,128)} async-done(((f32[10,8,256]{2,1,0:T(8,128)}), f32[10,256,256]{2,1,0:T(8,128)}) %all-gather.10.cloned.1.call-update) | async-done | bytes 2621456 | tf_op jit(solution)/shard_map/all_gather | solution.py:89
  545.2 103.2 %reduce-scatter.7.cloned.1.call-done = f32[16,256]{1,0:T(8,128)} async-done(((f32[512,256]{1,0:T(8,128)}), f32[16,256]{1,0:T(8,128)}) %reduce-scatter.7.cloned.1.call-update) | async-done | bytes 16400 | tf_op jit(solution)/shard_map/reduce_scatter | solution.py:52
  654.2 102.5 %reduce-scatter.5.cloned.1.call-done = f32[16,256]{1,0:T(8,128)} async-done(((f32[512,256]{1,0:T(8,128)}), f32[16,256]{1,0:T(8,128)}) %reduce-scatter.5.cloned.1.call-update) | async-done | bytes 16400 | tf_op jit(solution)/shard_map/reduce_scatter | solution.py:52
  760.5 1.9 pad_maximum_fusion.2
  764.3 65.2 %all-gather.12.cloned.1.call-done = f32[10,256,256]{2,1,0:T(8,128)} async-done(((f32[10,8,256]{2,1,0:T(8,128)}), f32[10,256,256]{2,1,0:T(8,128)}) %all-gather.12.cloned.1.call-update) | async-done | bytes 2621456 | tf_op jit(solution)/shard_map/all_gather | solution.py:90
  829.5 417.1 %all-reduce.5.cloned.1.call-done = (f32[2,256,256]{2,1,0:T(8,128)}, f32[3,256,256]{2,1,0:T(8,128)}, f32[4,256,256]{2,1,0:T(8,128)}, f32[1,256,256]{2,1,0:T(8,128)}) async-done(((f32[2,256,256]{2,1,0:T(8,128)}, f32[3,256,256]{2,1,0:T(8,128)}, f32[4,256,256]{2,1,0:T(8,128)}, f32[1,256,256]{2,1,0:T(8,128)}), (f32[2,256,256]{2,1,0:T(8,128)}, f32[3,256,256]{2,1,0:T(8,128)}, f32[4,256,256]{2,1,0:T(8,128)}, ...) | async-done | bytes 2621456 | tf_op jit(solution)/shard_map/psum | solution.py:137
  1246.6 1.5 fusion.18
  1249.5 1.5 fusion.66
  1254.0 1.6 fusion.7
  1258.0 1.5 fusion.5
  1261.3 1.5 fusion.6
  1264.8 1.6 convolution_subtract_fusion.11
  1269.2 1.8 copy.38
  1271.0 1.5 fusion.1
  1272.5 1.5 fusion.2
  1279.8 1.6 convolution_subtract_fusion.6
  (162 shorter events, 56.1 us)
Async XLA Ops:
  8.0 242.9 %all-reduce.7.cloned.1.call-start = ((), (), s32[]{:S(2)}) async-start(), calls=%async_computation.12 | async-start | bytes 2097152 | tf_op jit(solution)/shard_map/psum | solution.py:13
  9.0 128.2 %copy-start.19 = (f32[2,1,256,1,1,256]{5,4,3,2,1,0:T(1,128)S(1)}, f32[2,1,256,1,1,256]{5,4,3,2,1,0:T(1,128)}, u32[]{:S(2)}) copy-start(f32[2,1,256,1,1,256]{5,4,3,2,1,0:T(1,128)} %param.6) | copy-start | bytes 1572868
  136.6 124.5 %all-gather.8.cloned.1.call-start = ((), (), s32[]{:S(2)}) async-start(), calls=%async_computation.8 | async-start | bytes 1081344 | tf_op jit(solution)/shard_map/all_gather | solution.py:91
  137.1 223.8 %reduce-scatter.11.cloned.1.call-start = ((), (), s32[]{:S(2)}) async-start(), calls=%async_computation.7 | async-start | bytes 540672 | tf_op jit(solution)/shard_map/reduce_scatter | solution.py:52
  250.9 5.5 copy-start.24
  253.7 215.4 %reduce-scatter.9.cloned.1.call-start = ((), (), s32[]{:S(2)}) async-start(), calls=%async_computation.6 | async-start | bytes 540672 | tf_op jit(solution)/shard_map/reduce_scatter | solution.py:52
  253.7 4.6 copy-start.23
  255.6 285.9 %all-gather.10.cloned.1.call-start = ((), (), s32[]{:S(2)}) async-start(), calls=%async_computation.9 | async-start | bytes 2703360 | tf_op jit(solution)/shard_map/all_gather | solution.py:89
  256.3 392.1 %reduce-scatter.7.cloned.1.call-start = ((), (), s32[]{:S(2)}) async-start(), calls=%async_computation.5 | async-start | bytes 540672 | tf_op jit(solution)/shard_map/reduce_scatter | solution.py:52
  256.4 4.6 copy-start.27
  257.0 3.9 copy-start.26
  258.2 498.6 %reduce-scatter.5.cloned.1.call-start = ((), (), s32[]{:S(2)}) async-start(), calls=%async_computation.4 | async-start | bytes 540672 | tf_op jit(solution)/shard_map/reduce_scatter | solution.py:52
  260.1 569.4 %all-gather.12.cloned.1.call-start = ((), (), s32[]{:S(2)}) async-start(), calls=%async_computation.10 | async-start | bytes 2703360 | tf_op jit(solution)/shard_map/all_gather | solution.py:90
  260.7 985.9 %all-reduce.5.cloned.1.call-start = ((), (), s32[]{:S(2)}) async-start(), calls=%async_computation.11 | async-start | bytes 5242880 | tf_op jit(solution)/shard_map/psum | solution.py:137
  541.4 215.3 %copy-start = (f32[10,256,256]{2,1,0:T(8,128)S(1)}, f32[10,256,256]{2,1,0:T(8,128)}, u32[]{:S(2)}) copy-start(f32[10,256,256]{2,1,0:T(8,128)} %all-gather.10.cloned.1.call-done) | copy-start | bytes 7864324
  1251.1 5.0 copy-start.1
  1258.0 5.4 copy-start.2
  1259.6 5.2 copy-start.20
  1261.3 5.7 copy-start.7
  1271.0 3.9 copy-start.3
  1271.0 4.3 copy-start.5
  1275.2 6.8 copy-start.14
  1276.7 4.7 copy-start.17
  1279.7 3.9 copy-start.13
  (13 other events, 35.4 us)
Sparse Core Ops, SparseCore 0:
  136.7 114.1 all-reduce.6
  763.6 482.9 all-reduce.4
Sparse Core Ops, SparseCore 1:
  139.2 67.6 all-gather.7
  253.7 107.1 reduce-scatter.10
  363.8 105.2 reduce-scatter.8
  471.2 70.2 all-gather.9
  544.2 104.1 reduce-scatter.6
  651.4 105.3 reduce-scatter.4
  758.8 70.6 all-gather.11
where the time goes:
time: 1300 us; the launch traced here: 1290 us
  waiting for transfers between devices  1080 us (83%)
  blocking collectives  125 us (10%)
  matrix products  53.2 us (4%)
  between operations  16.7 us (1%)
    psum x1, waiting for transfers between devices, per_device(): summed = lax.psum(local_gram, ('prow', 'pcol'))  417 us
    reduce_scatter x4, waiting for transfers between devices, reduce_one(): lax.psum_scatter(term(jnp.int32(0), lax.axis_size('pcol') * count), 'pcol...  410 us
    all_gather x4, blocking collectives, rows_one(): return lax.all_gather(piece, 'pcol', axis=1, tiled=True)  125 us
    psum x1, waiting for transfers between devices, from_root(): return lax.psum(jnp.where(mine, array, jnp.zeros_like(array)), axis)  114 us
    all_gather x1, waiting for transfers between devices, per_device(): lax.all_gather(factor_top, 'pcol', axis=1, tiled=True)  72.4 us
    all_gather x1, waiting for transfers between devices, per_device(): lax.all_gather(adjoint_top, 'pcol', axis=1, tiled=True)  65.2 us
    dot_general x30, matrix products, matmul(): jnp.dot(left, right, precision=HIGHEST, preferred_element_type=jnp.float32)  27.1 us
  transfers between devices with their start and end apart: 9, of which 8 were waited for; matrix products, arithmetic and copies ran while one was open for 2% of the time, Pallas kernels for 0%

commit v1 on v0

--- a/solution.py
+++ b/solution.py
@@ -87,7 +87,9 @@
     columns = low_factor.reshape(local_rows, K, NB)
     top_factor, top_adjoint, inverses = (
         lax.all_gather(factor_top, "pcol", axis=1, tiled=True),
-        lax.all_gather(adjoint_top, "pcol", axis=1, tiled=True),
+        jnp.concatenate(
+            lax.all_to_all(jnp.stack([adjoint_top] * lax.axis_size("pcol")), "pcol", 0, 0), axis=1
+        ),
         lax.all_gather(diag_inverse, "pcol", axis=1, tiled=True),
     )
     lower_grads = [None] * K

time: 1300 us -> 1340 us (1.031)
  waiting for transfers between devices: 1080 us -> 1110 us
    all_gather x1 -> x0, waiting for transfers between devices: 65.2 us -> none  [per_device(): lax.all_gather(adjoint_top, 'pcol', axis=1, tiled=True)]
    psum x1, waiting for transfers between devices: 417 us -> 481 us  [per_device(): summed = lax.psum(local_gram, ('prow', 'pcol'))]
    reduce_scatter x4, waiting for transfers between devices: 410 us -> 444 us  [reduce_one(): lax.psum_scatter(term(jnp.int32(0), lax.axis_size('pcol') * count), 'pcol...]
  transfers between devices with their start and end apart: 9 -> 9, of which waited for: 8 -> 7; matrix products, arithmetic and copies ran while one was open for 2% -> 2% of each run, Pallas kernels for 0% -> 0%
where the time goes in v1:
time: 1340 us
  waiting for transfers between devices  1110 us (83%)
  blocking collectives  125 us (9%)
  matrix products  51.6 us (4%)
  between operations  16.9 us (1%)
    psum x1, waiting for transfers between devices, per_device(): summed = lax.psum(local_gram, ('prow', 'pcol'))  481 us
    reduce_scatter x4, waiting for transfers between devices, reduce_one(): lax.psum_scatter(term(jnp.int32(0), lax.axis_size('pcol') * count), 'pcol...  444 us
    all_gather x4, blocking collectives, rows_one(): return lax.all_gather(piece, 'pcol', axis=1, tiled=True)  125 us
    psum x1, waiting for transfers between devices, from_root(): return lax.psum(jnp.where(mine, array, jnp.zeros_like(array)), axis)  114 us
    all_gather x1, waiting for transfers between devices, per_device(): lax.all_gather(factor_top, 'pcol', axis=1, tiled=True)  72.8 us
    dot_general x30, matrix products, matmul(): jnp.dot(left, right, precision=HIGHEST, preferred_element_type=jnp.float32)  26.9 us
  transfers between devices with their start and end apart: 9, of which 7 were waited for; matrix products, arithmetic and copies ran while one was open for 2% of the time, Pallas kernels for 0%

profile of v1, /device:TPU:8, one launch (start us, length us, event | category | flops | bytes accessed | tf_op | source)
XLA Modules:
  0.0 1339.0 jit_solution(2556677705316282470)
XLA Ops:
  9.0 37.8 %all-gather.3 = f32[2,256,256]{2,1,0:T(8,128)S(1)} all-gather(f32[2,8,256]{2,1,0:T(8,128)S(1)} %get-tuple-element.15), channel_id=5, replica_groups=mesh['prow'=16,'pcol'=32] {'pcol'}, dimensions={1}, use_global_device_ids=true | all-gather | bytes 540672 | tf_op jit(solution)/shard_map/all_gather | solution.py:44
  46.8 28.5 %all-gather.2 = f32[2,256,256]{2,1,0:T(8,128)S(1)} all-gather(f32[2,8,256]{2,1,0:T(8,128)S(1)} %get-tuple-element.16), channel_id=4, replica_groups=mesh['prow'=16,'pcol'=32] {'pcol'}, dimensions={1}, use_global_device_ids=true | all-gather | bytes 540672 | tf_op jit(solution)/shard_map/all_gather | solution.py:44
  76.7 29.8 %all-gather.1 = f32[2,256,256]{2,1,0:T(8,128)S(1)} all-gather(f32[2,8,256]{2,1,0:T(8,128)S(1)} %get-tuple-element.17), channel_id=3, replica_groups=mesh['prow'=16,'pcol'=32] {'pcol'}, dimensions={1}, use_global_device_ids=true | all-gather | bytes 540672 | tf_op jit(solution)/shard_map/all_gather | solution.py:44
  107.3 28.5 %all-gather = f32[2,256,256]{2,1,0:T(8,128)S(1)} all-gather(f32[2,8,256]{2,1,0:T(8,128)S(1)} %get-tuple-element.14), channel_id=2, replica_groups=mesh['prow'=16,'pcol'=32] {'pcol'}, dimensions={1}, use_global_device_ids=true | all-gather | bytes 540672 | tf_op jit(solution)/shard_map/all_gather | solution.py:44
  137.2 113.6 %all-reduce.7.cloned.1.call-done = (f32[256,256]{1,0:T(8,128)}, f32[256,256]{1,0:T(8,128)}, f32[256,256]{1,0:T(8,128)}, f32[256,256]{1,0:T(8,128)}) async-done(((f32[256,256]{1,0:T(8,128)}, f32[256,256]{1,0:T(8,128)}, f32[256,256]{1,0:T(8,128)}, f32[256,256]{1,0:T(8,128)}), (f32[256,256]{1,0:T(8,128)}, f32[256,256]{1,0:T(8,128)}, f32[256,256]{1,0:T(8,128)}, ...) | async-done | bytes 1048592 | tf_op jit(solution)/shard_map/psum | solution.py:13
  250.8 1.6 convolution_bitcast_fusion
  256.2 1.8 stack.65
  258.0 12.8 all-to-all-start
  274.9 126.3 %reduce-scatter.11.cloned.1.call-done = f32[16,256]{1,0:T(8,128)} async-done(((f32[512,256]{1,0:T(8,128)}), f32[16,256]{1,0:T(8,128)}) %reduce-scatter.11.cloned.1.call-update) | async-done | bytes 16400 | tf_op jit(solution)/shard_map/reduce_scatter | solution.py:52
  405.2 112.0 %reduce-scatter.9.cloned.1.call-done = f32[16,256]{1,0:T(8,128)} async-done(((f32[512,256]{1,0:T(8,128)}), f32[16,256]{1,0:T(8,128)}) %reduce-scatter.9.cloned.1.call-update) | async-done | bytes 16400 | tf_op jit(solution)/shard_map/reduce_scatter | solution.py:52
  517.2 72.8 %all-gather.9.cloned.1.call-done = f32[10,256,256]{2,1,0:T(8,128)} async-done(((f32[10,8,256]{2,1,0:T(8,128)}), f32[10,256,256]{2,1,0:T(8,128)}) %all-gather.9.cloned.1.call-update) | async-done | bytes 2621456 | tf_op jit(solution)/shard_map/all_gather | solution.py:89
  593.4 103.8 %reduce-scatter.7.cloned.1.call-done = f32[16,256]{1,0:T(8,128)} async-done(((f32[512,256]{1,0:T(8,128)}), f32[16,256]{1,0:T(8,128)}) %reduce-scatter.7.cloned.1.call-update) | async-done | bytes 16400 | tf_op jit(solution)/shard_map/reduce_scatter | solution.py:52
  703.8 101.6 %reduce-scatter.5.cloned.1.call-done = f32[16,256]{1,0:T(8,128)} async-done(((f32[512,256]{1,0:T(8,128)}), f32[16,256]{1,0:T(8,128)}) %reduce-scatter.5.cloned.1.call-update) | async-done | bytes 16400 | tf_op jit(solution)/shard_map/reduce_scatter | solution.py:52
  810.0 480.7 %all-reduce.5.cloned.1.call-done = (f32[2,256,256]{2,1,0:T(8,128)}, f32[3,256,256]{2,1,0:T(8,128)}, f32[4,256,256]{2,1,0:T(8,128)}, f32[256,256]{1,0:T(8,128)}) async-done(((f32[2,256,256]{2,1,0:T(8,128)}, f32[3,256,256]{2,1,0:T(8,128)}, f32[4,256,256]{2,1,0:T(8,128)}, f32[256,256]{1,0:T(8,128)}), (f32[2,256,256]{2,1,0:T(8,128)}, f32[3,256,256]{2,1,0:T(8,128)}, f32[4,256,256]{2,1,0:T(8,128)}, ...) | async-done | bytes 2621456 | tf_op jit(solution)/shard_map/psum | solution.py:139
  1290.7 1.6 fusion.19
  1293.6 1.5 fusion.67
  1298.2 1.6 fusion.7
  1302.2 1.5 fusion.5
  1305.5 1.5 fusion.6
  1309.0 1.6 convolution_subtract_fusion.11
  1313.4 1.8 copy.56
  1315.2 1.5 fusion.1
  1316.7 1.5 fusion.2
  1324.0 1.6 convolution_subtract_fusion.6
  (165 shorter events, 54.5 us)
Async XLA Ops:
  8.0 242.8 %all-reduce.7.cloned.1.call-start = ((), (), s32[]{:S(2)}) async-start(), calls=%async_computation.12 | async-start | bytes 2097152 | tf_op jit(solution)/shard_map/psum | solution.py:13
  9.0 128.2 %copy-start.19 = (f32[2,1,256,1,1,256]{5,4,3,2,1,0:T(1,128)S(1)}, f32[2,1,256,1,1,256]{5,4,3,2,1,0:T(1,128)}, u32[]{:S(2)}) copy-start(f32[2,1,256,1,1,256]{5,4,3,2,1,0:T(1,128)} %param.6) | copy-start | bytes 1572868
  136.5 138.4 %all-gather.7.cloned.1.call-start = ((), (), s32[]{:S(2)}) async-start(), calls=%async_computation.9 | async-start | bytes 1081344 | tf_op jit(solution)/shard_map/all_gather | solution.py:93
  137.1 264.2 %reduce-scatter.11.cloned.1.call-start = ((), (), s32[]{:S(2)}) async-start(), calls=%async_computation.8 | async-start | bytes 540672 | tf_op jit(solution)/shard_map/reduce_scatter | solution.py:52
  250.8 5.4 copy-start.27
  253.6 263.6 %reduce-scatter.9.cloned.1.call-start = ((), (), s32[]{:S(2)}) async-start(), calls=%async_computation.7 | async-start | bytes 540672 | tf_op jit(solution)/shard_map/reduce_scatter | solution.py:52
  255.5 334.6 %all-gather.9.cloned.1.call-start = ((), (), s32[]{:S(2)}) async-start(), calls=%async_computation.10 | async-start | bytes 2703360 | tf_op jit(solution)/shard_map/all_gather | solution.py:89
  258.0 12.9 copy-start.24
  258.0 1032.7 %all-to-all-start = ((f32[32,10,8,256]{3,2,1,0:T(8,128)}), f32[32,10,8,256]{3,2,1,0:T(8,128)}, u32[]{:S(2)}, u32[]{:S(2)}) async-start(f32[32,10,8,256]{3,2,1,0:T(8,128)} %stack.65), calls=%async_computation.4 | async-start | bytes 5242880 | tf_op jit(solution)/shard_map/all_to_all | solution.py:91
  270.9 426.3 %reduce-scatter.7.cloned.1.call-start = ((), (), s32[]{:S(2)}) async-start(), calls=%async_computation.6 | async-start | bytes 540672 | tf_op jit(solution)/shard_map/reduce_scatter | solution.py:52
  272.7 532.7 %reduce-scatter.5.cloned.1.call-start = ((), (), s32[]{:S(2)}) async-start(), calls=%async_computation.5 | async-start | bytes 540672 | tf_op jit(solution)/shard_map/reduce_scatter | solution.py:52
  274.7 1016.0 %all-reduce.5.cloned.1.call-start = ((), (), s32[]{:S(2)}) async-start(), calls=%async_computation.11 | async-start | bytes 5242880 | tf_op jit(solution)/shard_map/psum | solution.py:139
  591.2 214.2 %copy-start = (f32[10,256,256]{2,1,0:T(8,128)S(1)}, f32[10,256,256]{2,1,0:T(8,128)}, u32[]{:S(2)}) copy-start(f32[10,256,256]{2,1,0:T(8,128)} %all-gather.9.cloned.1.call-done) | copy-start | bytes 7864324
  1295.3 5.0 copy-start.1
  1302.2 5.4 copy-start.2
  1303.8 5.2 copy-start.20
  1305.5 5.6 copy-start.7
  1315.2 3.9 copy-start.3
  1315.2 4.3 copy-start.5
  1319.4 6.8 copy-start.14
  1320.5 3.5 copy-start.22
  1320.9 4.7 copy-start.17
  1323.9 3.9 copy-start.13
  1327.4 3.3 copy-start.12
  (14 other events, 34.5 us)
Sparse Core Ops, SparseCore 0:
  136.6 114.1 all-reduce.6
  809.3 481.3 all-reduce.4
Sparse Core Ops, SparseCore 1:
  139.1 67.6 all-gather.6
  253.7 147.5 reduce-scatter.10
  404.1 113.0 reduce-scatter.8
  519.4 70.6 all-gather.8
  592.8 104.3 reduce-scatter.6
  700.3 105.1 reduce-scatter.4
